TPU v7x, 32 devices: a whole 2x2x4 slice. The times are simulated.
32 devices in a mesh: ctx: 4 (over z), head: 8 (over y, x, core).
Axes of the slice: x: 2, y: 2, z: 4, core: 2. Of those that a mesh axis runs over, the one named last changes fastest.
Arguments:
- query_rows: bfloat16 [8192, 4096], P('ctx', 'head'), may hold values from -6 to 6
- key_rows: bfloat16 [8192, 4096], P('ctx', 'head'), may hold values from -6 to 6
- value_rows: bfloat16 [8192, 4096], P('ctx', 'head'), may hold values from -6 to 6
- out_grad: bfloat16 [8192, 4096], P('ctx', 'head'), may hold values from -6 to 6
- hub_blocks: int32 [2], replicated, may hold values from 0 to 63, as said below
- local_lists: int32 [64, 6], replicated, may hold values from -3 to 3
Outputs:
- attended: bfloat16 [8192, 4096], P('ctx', 'head')
- query_gradient: bfloat16 [8192, 4096], P('ctx', 'head')
- key_grad: bfloat16 [8192, 4096], P('ctx', 'head')
- value_grad: bfloat16 [8192, 4096], P('ctx', 'head')
Inputs may be any that keep to these rules, and one draw needn't show every extreme that they name: `hub_blocks`: 2 distinct block numbers.
All inputs are finite; a program needn't handle non-finite values.
Results may differ from a plain program's by a relative error of at most 0.012.
The roundings to bfloat16 on the way count: a program that leaves them out, or rounds other values in their place, can miss the bound.
Values may be sent and summed in bfloat16 or wider, within the bound.
A program may use at most 192 MiB of HBM per device.

v0:
```python
import math
import jax
import jax.numpy as jnp
from jax import lax
from jax.sharding import PartitionSpec as P

DH = 128
BLK = 128
HB = 3
G = 2


def padded_2(cells, sides, width):
    for axis, dim in sides:
        count = lax.axis_size(axis)
        ends = count - 1
        head = lax.slice_in_dim(cells, 0, width, axis=dim)
        tail = lax.slice_in_dim(cells, cells.shape[dim] - width, cells.shape[dim], axis=dim)
        cells = jnp.concatenate(
            [
                lax.ppermute(tail, axis, [(i, (i + 1) % count) for i in range(ends)]),
                cells,
                lax.ppermute(head, axis, [((i + 1) % count, i) for i in range(ends)]),
            ],
            axis=dim,
        )
    return cells


def entry_table(block_lists, positions, first_block, total_blocks, extended):
    global_block = first_block - HB + positions
    query_inside = (global_block >= 0) & (global_block < total_blocks)
    key_spot = positions[:, None] + block_lists
    key_global = global_block[:, None] + block_lists
    living = query_inside[:, None] & (key_global >= 0) & (key_global < total_blocks)
    living = living & (key_spot >= 0) & (key_spot < extended)
    set_count = positions.shape[0]
    hub_spots = jnp.broadcast_to(extended + jnp.arange(G, dtype=jnp.int32)[None, :], (set_count, G))
    entries = jnp.concatenate([jnp.clip(key_spot, 0, extended - 1), hub_spots], axis=1)
    all_living = jnp.concatenate(
        [living, jnp.broadcast_to(query_inside[:, None], (set_count, G))], axis=1
    )
    return (entries, all_living)


def grouped(source):
    return source.reshape((source.shape[0] // 4, 4) + source.shape[1:])


def block_scores(query_group, entries, living, key_store, score_scale):
    gathered = key_store[entries]
    logit_scores = (
        jnp.einsum("bqhd,bekhd->bhqek", query_group, gathered, preferred_element_type=jnp.float32)
        * score_scale
    )
    logit_scores = jnp.where(living[:, None, None, :, None], logit_scores, -1e30)
    return (logit_scores, gathered)


def local(query_rows, key_rows, value_rows, out_grad, hub_blocks, local_lists):
    score_scale = 1.0 / math.sqrt(DH)
    ctx_count = lax.axis_size("ctx")
    position = lax.axis_index("ctx")
    tok_rows, columns = query_rows.shape
    head_count = columns // DH
    blocks_here = tok_rows // BLK
    total_blocks = blocks_here * ctx_count
    extended = blocks_here + 2 * HB
    first_block = position * blocks_here
    padded_lists = jnp.pad(local_lists, ((HB, HB), (0, 0)))
    ext_lists = lax.dynamic_slice_in_dim(padded_lists, first_block, extended, 0)
    positions = jnp.arange(extended, dtype=jnp.int32)
    joined = jnp.concatenate([key_rows, value_rows], axis=1)
    widened = padded_2(joined, (("ctx", 0),), HB * BLK)
    far_keys = widened[:, :columns]
    far_values = widened[:, columns : 2 * columns]
    hub_spot = hub_blocks - first_block
    hub_picks = hub_spot[:, None] == jnp.arange(blocks_here, dtype=jnp.int32)[None, :]
    hub_term = jnp.dot(
        hub_picks.astype(jnp.bfloat16),
        joined.reshape(blocks_here, BLK * 2 * columns),
        preferred_element_type=jnp.float32,
    )
    hub_store = lax.psum(hub_term.astype(jnp.bfloat16), "ctx").reshape(G * BLK, 2 * columns)
    key_store = jnp.concatenate([far_keys, hub_store[:, :columns]], axis=0).reshape(
        extended + G, BLK, head_count, DH
    )
    value_store = jnp.concatenate([far_values, hub_store[:, columns:]], axis=0).reshape(
        extended + G, BLK, head_count, DH
    )
    local_entries, local_living = entry_table(
        ext_lists[HB : HB + blocks_here],
        positions[HB : HB + blocks_here],
        first_block,
        total_blocks,
        extended,
    )
    query_blocks = query_rows.reshape(blocks_here, BLK, head_count, DH)
    grad_blocks = out_grad.reshape(blocks_here, BLK, head_count, DH)

    def forward_group(members):
        query_group, entries, living = members
        logit_scores, gathered = block_scores(query_group, entries, living, key_store, score_scale)
        highest = jnp.max(logit_scores, axis=(3, 4), keepdims=True)
        log_norm = highest + jnp.log(
            jnp.sum(jnp.exp(logit_scores - highest), axis=(3, 4), keepdims=True)
        )
        weights = jnp.exp(logit_scores - log_norm).astype(jnp.bfloat16)
        mixed = jnp.einsum(
            "bhqek,bekhd->bqhd", weights, value_store[entries], preferred_element_type=jnp.float32
        )
        return (mixed.astype(jnp.bfloat16), log_norm[:, :, :, 0, 0])

    mixed, norms = lax.map(
        forward_group, (grouped(query_blocks), grouped(local_entries), grouped(local_living))
    )
    attended = mixed.reshape(tok_rows, columns)
    log_norms = norms.reshape(blocks_here, head_count, BLK)
    offsets = jnp.sum(
        grad_blocks.astype(jnp.float32)
        * attended.reshape(blocks_here, BLK, head_count, DH).astype(jnp.float32),
        axis=3,
    )
    offsets = jnp.transpose(offsets, (0, 2, 1))
    set_norms, set_offsets = (log_norms, offsets)
    set_queries, set_grads = (query_blocks, grad_blocks)
    set_entries, set_living = (local_entries, local_living)
    store_rows = extended + G
    store_ids = jnp.arange(store_rows, dtype=jnp.int32)

    def grad_group(carry, members):
        key_acc, value_acc = carry
        query_group, pushed_rows, norm_group, offset_group, entries, living = members
        logit_scores, gathered = block_scores(query_group, entries, living, key_store, score_scale)
        chances = jnp.exp(logit_scores - norm_group[:, :, :, None, None])
        weights = chances.astype(jnp.bfloat16)
        shifted_entries = jnp.einsum(
            "bqhd,bekhd->bhqek",
            pushed_rows,
            value_store[entries],
            preferred_element_type=jnp.float32,
        )
        decay_slopes = (
            chances * (shifted_entries - offset_group[:, :, :, None, None]) * score_scale
        ).astype(jnp.bfloat16)
        query_part = jnp.einsum(
            "bhqek,bekhd->bqhd", decay_slopes, gathered, preferred_element_type=jnp.float32
        )
        key_part = jnp.einsum(
            "bhqek,bqhd->bekhd", decay_slopes, query_group, preferred_element_type=jnp.float32
        )
        value_part = jnp.einsum(
            "bhqek,bqhd->bekhd", weights, pushed_rows, preferred_element_type=jnp.float32
        )
        spots = (
            ((entries[:, :, None] == store_ids[None, None, :]) & living[:, :, None])
            .astype(jnp.float32)
            .reshape(-1, store_rows)
        )
        key_acc = key_acc + jnp.dot(
            spots.T, key_part.reshape(spots.shape[0], -1), precision=lax.Precision.HIGHEST
        )
        value_acc = value_acc + jnp.dot(
            spots.T, value_part.reshape(spots.shape[0], -1), precision=lax.Precision.HIGHEST
        )
        return ((key_acc, value_acc), query_part)

    empty_acc = jnp.zeros((store_rows, BLK * columns), jnp.float32)
    (key_acc, value_acc), query_parts = lax.scan(
        grad_group,
        (empty_acc, empty_acc),
        (
            grouped(set_queries),
            grouped(set_grads),
            grouped(set_norms),
            grouped(set_offsets),
            grouped(set_entries),
            grouped(set_living),
        ),
    )
    query_gradient = (
        query_parts.reshape(-1, BLK, head_count, DH).reshape(tok_rows, columns).astype(jnp.bfloat16)
    )
    gradients = jnp.concatenate([key_acc, value_acc], axis=1)
    owned_rows = gradients[HB : HB + blocks_here]
    rim_rows = jnp.concatenate([gradients[:HB], gradients[HB + blocks_here : extended]], axis=0)
    returned = padded_2(rim_rows.astype(jnp.bfloat16), (("ctx", 0),), HB).astype(rim_rows.dtype)
    owned_rows = owned_rows.at[:HB].add(returned[:HB])
    owned_rows = owned_rows.at[blocks_here - HB :].add(returned[3 * HB :])
    hub_total = lax.psum(gradients[extended : extended + G], "ctx")
    owned_rows = owned_rows + jnp.dot(
        hub_picks.T.astype(jnp.float32), hub_total, precision=lax.Precision.HIGHEST
    )
    key_grad = owned_rows[:, : BLK * columns].reshape(tok_rows, columns).astype(jnp.bfloat16)
    value_grad = owned_rows[:, BLK * columns :].reshape(tok_rows, columns).astype(jnp.bfloat16)
    return (attended, query_gradient, key_grad, value_grad)


def solution(mesh):
    return jax.shard_map(
        local,
        mesh=mesh,
        in_specs=(P("ctx", "head"), P("ctx", "head"), P("ctx", "head"), P("ctx", "head"), P(), P()),
        out_specs=(P("ctx", "head"), P("ctx", "head"), P("ctx", "head"), P("ctx", "head")),
        check_vma=False,
    )
```

profile of v0, /device:TPU:0, one launch (start us, length us, event | category | flops | bytes accessed | tf_op | source)
XLA Modules:
  0.0 707.2 jit_solution(10489579091226312188)
XLA Ops:
  44.7 26.4 %all-reduce.4.cloned.1.call-done = bf16[256,1024]{1,0:T(8,128)(2,1)} async-done(((bf16[256,1024]{1,0:T(8,128)(2,1)}), bf16[256,1024]{1,0:T(8,128)(2,1)}) %all-reduce.4.cloned.1.call-update) | async-done | bytes 524304 | tf_op jit(solution)/shard_map/psum | solution.py:84
  92.2 99.9 %while.29 = (s32[]{:T(128)}, bf16[4,4,128,4,128]{2,4,3,1,0:T(8,128)(2,1)}, f32[4,4,4,128]{3,2,1,0:T(4,128)S(1)}, s32[4,4,8]{2,1,0:T(4,128)S(1)}, bf16[24,128,4,1...) while((s32[]{:T(128)}, ...), condition=%wide.region_4.5_spmd, body=%wide.region_1.4_spmd.sunk | while | flops 1097071744 | bytes 76616880 | solution.py:114
  123.4 7.6 %gather_fusion = bf16[32,128,4,128]{3,2,1,0:T(4,128)(2,1)} fusion(bf16[24,128,4,128]{3,2,1,0:T(4,128)(2,1)} %get-tuple-element.451, s32[1024]{0:T(1024)S(1)} %pad_clamp_fusion.4), kind=kCustom, calls=%fused_computation.1.clone.1 | custom fusion | bytes 8388736 | tf_op jit(solution)/shard_map/while/body/eval_jaxpr/gather | solution.py:51
  195.7 394.1 %while.30 = (s32[]{:T(128)}, f32[24,65536]{1,0:T(8,128)}, f32[24,65536]{1,0:T(8,128)}, bf16[4,4,128,4,128]{2,4,3,1,0:T(8,128)(2,1)}, s32[4,4,8]{2,1,0:T(4,128)S(...) while((s32[]{:T(128)}, f32[24,65536]{1,0:T(8,128)}, ...), condition=%wide.region_7.8_spmd.clone, body=%wide.region_6.7_spmd.clone.sunk | while | flops 3921678336 | bytes 274790528 | solution.py:169
  233.1 9.9 %copy.107 = f32[4,8,128,4,128]{4,3,2,1,0:T(4,128)} copy(f32[4,8,128,4,128]{2,4,1,3,0:T(8,128)} %fusion.115) | data formatting | bytes 16777216 | tf_op jit(solution)/shard_map/while/body/eval_jaxpr/bhqek,bqhd->bekhd/transpose | solution.py:152
  243.0 9.0 %reshape.295 = f32[32,65536]{1,0:T(8,128)} reshape(f32[4,8,128,4,128]{4,3,2,1,0:T(4,128)} %copy.107) | data formatting | bytes 16777216 | tf_op jit(solution)/shard_map/while/body/eval_jaxpr/reshape | solution.py:164
  252.1 8.3 %convolution_add_fusion.6 = f32[24,65536]{1,0:T(8,128)} fusion(f32[32,65536]{1,0:T(8,128)} %reshape.295, f32[24,65536]{1,0:T(8,128)} %get-tuple-element.469, pred[]{:T(512)S(6)} %compare.14, s32[32]{0:T(128)S(1)} %eq.72, pred[32]{0:T(512)(128)(4,1)S(1)} %and.73), kind=kOutput, calls=%fused_computation.30.clone.1 | convolution fusion | flops 607127040 | bytes 20971680 | tf_op jit(solution)/shard_map/while/body/eval_jaxpr/dot_general | solution.py:163
  265.9 9.9 %copy.106 = f32[4,8,128,4,128]{4,3,2,1,0:T(4,128)} copy(f32[4,8,128,4,128]{2,4,1,3,0:T(8,128)} %convolution_bitcast_fusion.3) | data formatting | bytes 16777216 | tf_op jit(solution)/shard_map/while/body/eval_jaxpr/bhqek,bqhd->bekhd/transpose | solution.py:149
  275.8 9.0 %reshape.294 = f32[32,65536]{1,0:T(8,128)} reshape(f32[4,8,128,4,128]{4,3,2,1,0:T(4,128)} %copy.106) | data formatting | bytes 16777216 | tf_op jit(solution)/shard_map/while/body/eval_jaxpr/reshape | solution.py:161
  284.9 8.0 %convolution_add_fusion.5 = f32[24,65536]{1,0:T(8,128)} fusion(f32[32,65536]{1,0:T(8,128)} %reshape.294, f32[24,65536]{1,0:T(8,128)} %get-tuple-element.468, pred[]{:T(512)S(6)} %compare.14, s32[32]{0:T(128)S(1)} %eq.72, pred[32]{0:T(512)(128)(4,1)S(1)} %and.73), kind=kOutput, calls=%fused_computation.31.clone.1 | convolution fusion | flops 607127040 | bytes 20971680 | tf_op jit(solution)/shard_map/while/body/eval_jaxpr/dot_general | solution.py:160
  330.1 9.9 %copy.107 = f32[4,8,128,4,128]{4,3,2,1,0:T(4,128)} copy(f32[4,8,128,4,128]{2,4,1,3,0:T(8,128)} %fusion.115) | data formatting | bytes 16777216 | tf_op jit(solution)/shard_map/while/body/eval_jaxpr/bhqek,bqhd->bekhd/transpose | solution.py:152
  340.0 9.0 %reshape.295 = f32[32,65536]{1,0:T(8,128)} reshape(f32[4,8,128,4,128]{4,3,2,1,0:T(4,128)} %copy.107) | data formatting | bytes 16777216 | tf_op jit(solution)/shard_map/while/body/eval_jaxpr/reshape | solution.py:164
  349.0 9.2 %convolution_add_fusion.6 = f32[24,65536]{1,0:T(8,128)} fusion(f32[32,65536]{1,0:T(8,128)} %reshape.295, f32[24,65536]{1,0:T(8,128)} %get-tuple-element.469, pred[]{:T(512)S(6)} %compare.14, s32[32]{0:T(128)S(1)} %eq.72, pred[32]{0:T(512)(128)(4,1)S(1)} %and.73), kind=kOutput, calls=%fused_computation.30.clone.1 | convolution fusion | flops 607127040 | bytes 20971680 | tf_op jit(solution)/shard_map/while/body/eval_jaxpr/dot_general | solution.py:163
  363.8 9.9 %copy.106 = f32[4,8,128,4,128]{4,3,2,1,0:T(4,128)} copy(f32[4,8,128,4,128]{2,4,1,3,0:T(8,128)} %convolution_bitcast_fusion.3) | data formatting | bytes 16777216 | tf_op jit(solution)/shard_map/while/body/eval_jaxpr/bhqek,bqhd->bekhd/transpose | solution.py:149
  373.8 9.0 %reshape.294 = f32[32,65536]{1,0:T(8,128)} reshape(f32[4,8,128,4,128]{4,3,2,1,0:T(4,128)} %copy.106) | data formatting | bytes 16777216 | tf_op jit(solution)/shard_map/while/body/eval_jaxpr/reshape | solution.py:161
  382.8 9.0 %convolution_add_fusion.5 = f32[24,65536]{1,0:T(8,128)} fusion(f32[32,65536]{1,0:T(8,128)} %reshape.294, f32[24,65536]{1,0:T(8,128)} %get-tuple-element.468, pred[]{:T(512)S(6)} %compare.14, s32[32]{0:T(128)S(1)} %eq.72, pred[32]{0:T(512)(128)(4,1)S(1)} %and.73), kind=kOutput, calls=%fused_computation.31.clone.1 | convolution fusion | flops 607127040 | bytes 20971680 | tf_op jit(solution)/shard_map/while/body/eval_jaxpr/dot_general | solution.py:160
  429.0 9.9 %copy.107 = f32[4,8,128,4,128]{4,3,2,1,0:T(4,128)} copy(f32[4,8,128,4,128]{2,4,1,3,0:T(8,128)} %fusion.115) | data formatting | bytes 16777216 | tf_op jit(solution)/shard_map/while/body/eval_jaxpr/bhqek,bqhd->bekhd/transpose | solution.py:152
  438.9 9.0 %reshape.295 = f32[32,65536]{1,0:T(8,128)} reshape(f32[4,8,128,4,128]{4,3,2,1,0:T(4,128)} %copy.107) | data formatting | bytes 16777216 | tf_op jit(solution)/shard_map/while/body/eval_jaxpr/reshape | solution.py:164
  447.9 9.2 %convolution_add_fusion.6 = f32[24,65536]{1,0:T(8,128)} fusion(f32[32,65536]{1,0:T(8,128)} %reshape.295, f32[24,65536]{1,0:T(8,128)} %get-tuple-element.469, pred[]{:T(512)S(6)} %compare.14, s32[32]{0:T(128)S(1)} %eq.72, pred[32]{0:T(512)(128)(4,1)S(1)} %and.73), kind=kOutput, calls=%fused_computation.30.clone.1 | convolution fusion | flops 607127040 | bytes 20971680 | tf_op jit(solution)/shard_map/while/body/eval_jaxpr/dot_general | solution.py:163
  462.8 9.9 %copy.106 = f32[4,8,128,4,128]{4,3,2,1,0:T(4,128)} copy(f32[4,8,128,4,128]{2,4,1,3,0:T(8,128)} %convolution_bitcast_fusion.3) | data formatting | bytes 16777216 | tf_op jit(solution)/shard_map/while/body/eval_jaxpr/bhqek,bqhd->bekhd/transpose | solution.py:149
  472.7 9.0 %reshape.294 = f32[32,65536]{1,0:T(8,128)} reshape(f32[4,8,128,4,128]{4,3,2,1,0:T(4,128)} %copy.106) | data formatting | bytes 16777216 | tf_op jit(solution)/shard_map/while/body/eval_jaxpr/reshape | solution.py:161
  481.7 9.0 %convolution_add_fusion.5 = f32[24,65536]{1,0:T(8,128)} fusion(f32[32,65536]{1,0:T(8,128)} %reshape.294, f32[24,65536]{1,0:T(8,128)} %get-tuple-element.468, pred[]{:T(512)S(6)} %compare.14, s32[32]{0:T(128)S(1)} %eq.72, pred[32]{0:T(512)(128)(4,1)S(1)} %and.73), kind=kOutput, calls=%fused_computation.31.clone.1 | convolution fusion | flops 607127040 | bytes 20971680 | tf_op jit(solution)/shard_map/while/body/eval_jaxpr/dot_general | solution.py:160
  527.9 9.9 %copy.107 = f32[4,8,128,4,128]{4,3,2,1,0:T(4,128)} copy(f32[4,8,128,4,128]{2,4,1,3,0:T(8,128)} %fusion.115) | data formatting | bytes 16777216 | tf_op jit(solution)/shard_map/while/body/eval_jaxpr/bhqek,bqhd->bekhd/transpose | solution.py:152
  537.8 9.0 %reshape.295 = f32[32,65536]{1,0:T(8,128)} reshape(f32[4,8,128,4,128]{4,3,2,1,0:T(4,128)} %copy.107) | data formatting | bytes 16777216 | tf_op jit(solution)/shard_map/while/body/eval_jaxpr/reshape | solution.py:164
  546.8 9.2 %convolution_add_fusion.6 = f32[24,65536]{1,0:T(8,128)} fusion(f32[32,65536]{1,0:T(8,128)} %reshape.295, f32[24,65536]{1,0:T(8,128)} %get-tuple-element.469, pred[]{:T(512)S(6)} %compare.14, s32[32]{0:T(128)S(1)} %eq.72, pred[32]{0:T(512)(128)(4,1)S(1)} %and.73), kind=kOutput, calls=%fused_computation.30.clone.1 | convolution fusion | flops 607127040 | bytes 20971680 | tf_op jit(solution)/shard_map/while/body/eval_jaxpr/dot_general | solution.py:163
  561.6 9.9 %copy.106 = f32[4,8,128,4,128]{4,3,2,1,0:T(4,128)} copy(f32[4,8,128,4,128]{2,4,1,3,0:T(8,128)} %convolution_bitcast_fusion.3) | data formatting | bytes 16777216 | tf_op jit(solution)/shard_map/while/body/eval_jaxpr/bhqek,bqhd->bekhd/transpose | solution.py:149
  571.6 9.0 %reshape.294 = f32[32,65536]{1,0:T(8,128)} reshape(f32[4,8,128,4,128]{4,3,2,1,0:T(4,128)} %copy.106) | data formatting | bytes 16777216 | tf_op jit(solution)/shard_map/while/body/eval_jaxpr/reshape | solution.py:161
  580.6 9.0 %convolution_add_fusion.5 = f32[24,65536]{1,0:T(8,128)} fusion(f32[32,65536]{1,0:T(8,128)} %reshape.294, f32[24,65536]{1,0:T(8,128)} %get-tuple-element.468, pred[]{:T(512)S(6)} %compare.14, s32[32]{0:T(128)S(1)} %eq.72, pred[32]{0:T(512)(128)(4,1)S(1)} %and.73), kind=kOutput, calls=%fused_computation.31.clone.1 | convolution fusion | flops 607127040 | bytes 20971680 | tf_op jit(solution)/shard_map/while/body/eval_jaxpr/dot_general | solution.py:160
  617.9 8.4 %slice.127 = f32[16,131072]{1,0:T(8,128)} slice(f32[24,131072]{1,0:T(8,128)} %constant_dynamic-update-slice_fusion.2), slice={[3:19], [0:131072]} | slice | bytes 16777216 | tf_op jit(solution)/shard_map/slice | solution.py:185
  638.9 20.5 %scatter-add.6 = f32[16,131072]{1,0:T(8,128)} dynamic-update-slice(f32[16,131072]{1,0:T(8,128)} %slice.127, f32[3,131072]{1,0:T(4,128)S(1)} %convert_add_fusion, s32[]{:T(128)} %constant.122.clone.1, s32[]{:T(128)} %constant.122.clone.1) | dynamic-update-slice | bytes 3145732 | tf_op jit(solution)/shard_map/scatter-add | solution.py:188
  663.6 13.4 %scatter-add.9 = f32[16,131072]{1,0:T(8,128)} dynamic-update-slice(f32[16,131072]{1,0:T(8,128)} %scatter-add.6, f32[3,131072]{1,0:T(4,128)S(1)} %slice_add_fusion, s32[]{:T(128)} %constant.132.clone.1, s32[]{:T(128)} %constant.122.clone.1) | dynamic-update-slice | bytes 3145732 | tf_op jit(solution)/shard_map/scatter-add | solution.py:189
  677.1 9.4 %all-reduce.6.cloned.1.call-done = f32[2,131072]{1,0:T(2,128)} async-done(((f32[2,131072]{1,0:T(2,128)}), f32[2,131072]{1,0:T(2,128)}) %all-reduce.6.cloned.1.call-update) | async-done | bytes 1048592 | tf_op jit(solution)/shard_map/psum | solution.py:190
  (242 shorter events, 382.9 us)
Async XLA Ops:
  7.2 2.2 copy-start.8
  7.2 63.9 %all-reduce.4.cloned.1.call-start = ((), (), s32[]{:S(2)}) async-start(), calls=%async_computation | async-start | bytes 1048576 | tf_op jit(solution)/shard_map/psum | solution.py:84
  13.0 59.1 %collective-permute-start = (bf16[384,1024]{1,0:T(8,128)(2,1)}, bf16[384,1024]{1,0:T(8,128)(2,1)S(1)}, u32[]{:S(2)}, u32[]{:S(2)}) collective-permute-start(bf16[384,1024]{1,0:T(8,128)(2,1)} %get-tuple-element.282), channel_id=1, source_target_pairs={{0,8},{8,16},{16,24},{1,9},{9,17},{17,25},{2,10},{10,18},{18,26},{... | collective-permute-start | bytes 2359304 | tf_op jit(solution)/shard_map/ppermute | solution.py:21
  18.0 54.1 %collective-permute-start.1 = (bf16[384,1024]{1,0:T(8,128)(2,1)}, bf16[384,1024]{1,0:T(8,128)(2,1)}, u32[]{:S(2)}, u32[]{:S(2)}) collective-permute-start(bf16[384,1024]{1,0:T(8,128)(2,1)} %get-tuple-element.283), channel_id=1, source_target_pairs={{8,0},{16,8},{24,16},{9,1},{17,9},{25,17},{10,2},{18,10},{26,18},{... | collective-permute-start | bytes 2359304 | tf_op jit(solution)/shard_map/ppermute | solution.py:23
  19.3 4.8 copy-start.12
  24.1 5.0 copy-start.7
  29.1 657.4 %all-reduce.6.cloned.1.call-start = ((), (), s32[]{:S(2)}) async-start(), calls=%async_computation.1 | async-start | bytes 2097152 | tf_op jit(solution)/shard_map/psum | solution.py:190
  31.2 3.3 copy-start.9
  111.8 2.2 copy-start.3
  136.6 2.2 copy-start.3
  186.3 2.2 copy-start.3
  219.1 3.7 copy-start.4
  219.1 3.8 copy-start.5
  222.9 3.5 copy-start
  252.0 8.3 %copy-start.2 = (bf16[4,4,128,8,128]{4,2,3,1,0:T(8,128)(2,1)S(1)}, bf16[4,4,128,8,128]{4,2,3,1,0:T(8,128)(2,1)}, u32[]{:S(2)}) copy-start(bf16[4,4,128,8,128]{4,2,3,1,0:T(8,128)(2,1)} %copy-done.1) | copy-start | bytes 12582916 | tf_op jit(solution)/shard_map/while
  316.1 3.7 copy-start.4
  316.1 3.8 copy-start.5
  319.9 3.5 copy-start
  349.0 9.2 %copy-start.2 = (bf16[4,4,128,8,128]{4,2,3,1,0:T(8,128)(2,1)S(1)}, bf16[4,4,128,8,128]{4,2,3,1,0:T(8,128)(2,1)}, u32[]{:S(2)}) copy-start(bf16[4,4,128,8,128]{4,2,3,1,0:T(8,128)(2,1)} %copy-done.1) | copy-start | bytes 12582916 | tf_op jit(solution)/shard_map/while
  415.0 3.7 copy-start.4
  415.0 3.8 copy-start.5
  418.8 3.5 copy-start
  447.9 9.2 %copy-start.2 = (bf16[4,4,128,8,128]{4,2,3,1,0:T(8,128)(2,1)S(1)}, bf16[4,4,128,8,128]{4,2,3,1,0:T(8,128)(2,1)}, u32[]{:S(2)}) copy-start(bf16[4,4,128,8,128]{4,2,3,1,0:T(8,128)(2,1)} %copy-done.1) | copy-start | bytes 12582916 | tf_op jit(solution)/shard_map/while
  513.9 3.7 copy-start.4
  513.9 3.8 copy-start.5
  517.7 3.5 copy-start
  546.8 9.2 %copy-start.2 = (bf16[4,4,128,8,128]{4,2,3,1,0:T(8,128)(2,1)S(1)}, bf16[4,4,128,8,128]{4,2,3,1,0:T(8,128)(2,1)}, u32[]{:S(2)}) copy-start(bf16[4,4,128,8,128]{4,2,3,1,0:T(8,128)(2,1)} %copy-done.1) | copy-start | bytes 12582916 | tf_op jit(solution)/shard_map/while
  589.8 6.1 slice-start
  589.8 6.1 slice-start.1
  606.3 26.6 %collective-permute-start.2 = (bf16[3,131072]{1,0:T(4,128)(2,1)}, bf16[3,131072]{1,0:T(4,128)(2,1)S(1)}, u32[]{:S(2)}, u32[]{:S(2)}) collective-permute-start(bf16[3,131072]{1,0:T(4,128)(2,1)} %get-tuple-element.276), channel_id=1, source_target_pairs={{0,8},{8,16},{16,24},{1,9},{9,17},{17,25},{2,10},{10,18},{18,26},{... | collective-permute-start | bytes 2359304 | tf_op jit(solution)/shard_map/ppermute | solution.py:21
  610.0 24.7 %collective-permute-start.3 = (bf16[3,131072]{1,0:T(4,128)(2,1)}, bf16[3,131072]{1,0:T(4,128)(2,1)}, u32[]{:S(2)}, u32[]{:S(2)}) collective-permute-start(bf16[3,131072]{1,0:T(4,128)(2,1)} %get-tuple-element.277), channel_id=1, source_target_pairs={{8,0},{16,8},{24,16},{9,1},{17,9},{25,17},{10,2},{18,10},{26,18},{... | collective-permute-start | bytes 2359304 | tf_op jit(solution)/shard_map/ppermute | solution.py:23
  663.6 22.9 %copy-start.11 = (s32[2]{0:T(128)S(1)}, s32[2]{0:T(128)}, u32[]{:S(2)}) copy-start(s32[2]{0:T(128)} %copy-done.10) | copy-start | bytes 28
  (7 other events, 13.5 us)
Sparse Core Ops, SparseCore 0:
  29.2 41.8 all-reduce.3
  633.0 53.5 all-reduce.5
where the time goes:
time: 718 us; the launch traced here: 707 us
  local copies, waits for them, and re-layouts  424 us (59%)
  matrix products  183 us (25%)
  waiting for transfers between devices  37.7 us (5%)
  other arithmetic  35.4 us (5%)
  between operations  14.6 us (2%)
  starting transfers between devices  11.3 us (2%)
    gather x16, local copies, waits for them, and re-layouts, block_scores(): gathered = key_store[entries]  104 us
    transpose x4, local copies, waits for them, and re-layouts, grad_group(): jnp.einsum('bhqek,bqhd->bekhd', weights, pushed_rows, preferred_element_t...  39.6 us
    transpose x4, local copies, waits for them, and re-layouts, grad_group(): jnp.einsum('bhqek,bqhd->bekhd', decay_slopes, query_group, preferred_elem...  39.6 us
    reshape x4, local copies, waits for them, and re-layouts, grad_group(): value_part.reshape(spots.shape[0], -1)  36.2 us
    reshape x4, local copies, waits for them, and re-layouts, grad_group(): key_part.reshape(spots.shape[0], -1)  36.2 us
    dot_general x4, matrix products, grad_group(): jnp.dot(spots.T, value_part.reshape(spots.shape[0], -1), precision=lax.Pr...  35.9 us
    dot_general x4, matrix products, grad_group(): jnp.dot(spots.T, key_part.reshape(spots.shape[0], -1), precision=lax.Prec...  35.1 us
    psum x1, waiting for transfers between devices, local(): lax.psum(hub_term.astype(jnp.bfloat16), 'ctx').reshape(G * BLK, 2 * columns)  26.4 us
  transfers between devices with their start and end apart: 6, of which 3 were waited for; matrix products, arithmetic and copies ran while one was open for 13% of the time, Pallas kernels for 0%

commit v1 on v0

--- a/solution.py
+++ b/solution.py
@@ -81,7 +81,9 @@
         joined.reshape(blocks_here, BLK * 2 * columns),
         preferred_element_type=jnp.float32,
     )
-    hub_store = lax.psum(hub_term.astype(jnp.bfloat16), "ctx").reshape(G * BLK, 2 * columns)
+    hub_store = jnp.sum(
+        jax.lax.all_gather(hub_term.astype(jnp.bfloat16), axis_name="ctx"), 0
+    ).reshape(G * BLK, 2 * columns)
     key_store = jnp.concatenate([far_keys, hub_store[:, :columns]], axis=0).reshape(
         extended + G, BLK, head_count, DH
     )

time: 718 us -> 749 us (1.043)
  loops' own time: 1.26 us -> 12.5 us
  waiting for transfers between devices: 37.7 us -> 48 us
    psum x1 -> x0, waiting for transfers between devices: 26.4 us -> none  [local(): lax.psum(hub_term.astype(jnp.bfloat16), 'ctx').reshape(G * BLK, 2 * columns)]
    ppermute x2, waiting for transfers between devices: 1.85 us -> 23.1 us  [padded_2(): lax.ppermute(head, axis, [((i + 1) % count, i) for i in range(ends)])]
    ppermute x2, waiting for transfers between devices: 0.01 us -> 14.9 us  [padded_2(): lax.ppermute(tail, axis, [(i, (i + 1) % count) for i in range(ends)])]
    another operation x1, loops' own time: 0.68 us -> 12.2 us  [local(): lax.scan(grad_group, (empty_acc, empty_acc), (grouped(set_queries), group...]
  transfers between devices with their start and end apart: 6 -> 6, of which waited for: 3 -> 3; matrix products, arithmetic and copies ran while one was open for 13% -> 12% of each run, Pallas kernels for 0% -> 0%
where the time goes in v1:
time: 749 us; the launch traced here: 736 us
  local copies, waits for them, and re-layouts  426 us (57%)
  matrix products  183 us (24%)
  waiting for transfers between devices  48 us (6%)
  other arithmetic  41.6 us (6%)
  between operations  14.7 us (2%)
  loops' own time  12.5 us (2%)
  starting transfers between devices  9.72 us (1%)
    gather x16, local copies, waits for them, and re-layouts, block_scores(): gathered = key_store[entries]  104 us
    transpose x4, local copies, waits for them, and re-layouts, grad_group(): jnp.einsum('bhqek,bqhd->bekhd', decay_slopes, query_group, preferred_elem...  39.7 us
    transpose x4, local copies, waits for them, and re-layouts, grad_group(): jnp.einsum('bhqek,bqhd->bekhd', weights, pushed_rows, preferred_element_t...  39.7 us
    reshape x4, local copies, waits for them, and re-layouts, grad_group(): key_part.reshape(spots.shape[0], -1)  36.1 us
    reshape x4, local copies, waits for them, and re-layouts, grad_group(): value_part.reshape(spots.shape[0], -1)  36.1 us
    dot_general x4, matrix products, grad_group(): jnp.dot(spots.T, value_part.reshape(spots.shape[0], -1), precision=lax.Pr...  35.9 us
    dot_general x4, matrix products, grad_group(): jnp.dot(spots.T, key_part.reshape(spots.shape[0], -1), precision=lax.Prec...  35.1 us
    ppermute x2, waiting for transfers between devices, padded_2(): lax.ppermute(head, axis, [((i + 1) % count, i) for i in range(ends)])  23.1 us
  transfers between devices with their start and end apart: 6, of which 3 were waited for; matrix products, arithmetic and copies ran while one was open for 12% of the time, Pallas kernels for 0%

profile of v1, /device:TPU:0, one launch (start us, length us, event | category | flops | bytes accessed | tf_op | source)
XLA Modules:
  0.0 736.0 jit_solution(16459749163349200230)
XLA Ops:
  45.3 14.9 %collective-permute-done = bf16[384,1024]{1,0:T(8,128)(2,1)S(1)} collective-permute-done((bf16[384,1024]{1,0:T(8,128)(2,1)}, bf16[384,1024]{1,0:T(8,128)(2,1)S(1)}, u32[]{:S(2)}, u32[]{:S(2)}) %collective-permute-start) | collective-permute-done | bytes 786464 | tf_op jit(solution)/shard_map/ppermute | solution.py:21
  60.2 23.1 %collective-permute-done.1 = bf16[384,1024]{1,0:T(8,128)(2,1)} collective-permute-done((bf16[384,1024]{1,0:T(8,128)(2,1)}, bf16[384,1024]{1,0:T(8,128)(2,1)}, u32[]{:S(2)}, u32[]{:S(2)}) %collective-permute-start.1) | collective-permute-done | bytes 786464 | tf_op jit(solution)/shard_map/ppermute | solution.py:23
  112.7 99.7 %while.29 = (s32[]{:T(128)}, bf16[4,4,128,4,128]{2,4,3,1,0:T(8,128)(2,1)}, f32[4,4,4,128]{3,2,1,0:T(4,128)S(1)}, s32[4,4,8]{2,1,0:T(4,128)S(1)}, bf16[24,128,4,1...) while((s32[]{:T(128)}, ...), condition=%wide.region_4.5_spmd, body=%wide.region_1.4_spmd.sunk | while | flops 1097071744 | bytes 76616880 | solution.py:116
  216.0 405.4 %while.30 = (s32[]{:T(128)}, f32[24,65536]{1,0:T(8,128)}, f32[24,65536]{1,0:T(8,128)}, bf16[4,4,128,4,128]{2,4,3,1,0:T(8,128)(2,1)}, s32[4,4,8]{2,1,0:T(4,128)S(...) while((s32[]{:T(128)}, f32[24,65536]{1,0:T(8,128)}, ...), condition=%wide.region_7.8_spmd.clone, body=%wide.region_6.7_spmd.clone.sunk | while | flops 3921678336 | bytes 274790528 | solution.py:171
  264.8 9.9 %copy.124 = f32[4,8,128,4,128]{4,3,2,1,0:T(4,128)} copy(f32[4,8,128,4,128]{2,4,1,3,0:T(8,128)} %fusion.116) | data formatting | bytes 16777216 | tf_op jit(solution)/shard_map/while/body/eval_jaxpr/bhqek,bqhd->bekhd/transpose | solution.py:154
  274.8 9.0 %reshape.299 = f32[32,65536]{1,0:T(8,128)} reshape(f32[4,8,128,4,128]{4,3,2,1,0:T(4,128)} %copy.124) | data formatting | bytes 16777216 | tf_op jit(solution)/shard_map/while/body/eval_jaxpr/reshape | solution.py:166
  283.8 8.2 %convolution_add_fusion.6 = f32[24,65536]{1,0:T(8,128)} fusion(f32[32,65536]{1,0:T(8,128)} %reshape.299, f32[24,65536]{1,0:T(8,128)} %get-tuple-element.489, pred[]{:T(512)S(6)} %compare.14, s32[32]{0:T(128)S(1)} %eq.72, pred[32]{0:T(512)(128)(4,1)S(1)} %and.73), kind=kOutput, calls=%fused_computation.30.clone.1 | convolution fusion | flops 607127040 | bytes 20971680 | tf_op jit(solution)/shard_map/while/body/eval_jaxpr/dot_general | solution.py:165
  297.6 9.9 %copy.123 = f32[4,8,128,4,128]{4,3,2,1,0:T(4,128)} copy(f32[4,8,128,4,128]{2,4,1,3,0:T(8,128)} %convolution_bitcast_fusion.3) | data formatting | bytes 16777216 | tf_op jit(solution)/shard_map/while/body/eval_jaxpr/bhqek,bqhd->bekhd/transpose | solution.py:151
  307.5 9.0 %reshape.298 = f32[32,65536]{1,0:T(8,128)} reshape(f32[4,8,128,4,128]{4,3,2,1,0:T(4,128)} %copy.123) | data formatting | bytes 16777216 | tf_op jit(solution)/shard_map/while/body/eval_jaxpr/reshape | solution.py:163
  316.6 8.0 %convolution_add_fusion.5 = f32[24,65536]{1,0:T(8,128)} fusion(f32[32,65536]{1,0:T(8,128)} %reshape.298, f32[24,65536]{1,0:T(8,128)} %get-tuple-element.488, pred[]{:T(512)S(6)} %compare.14, s32[32]{0:T(128)S(1)} %eq.72, pred[32]{0:T(512)(128)(4,1)S(1)} %and.73), kind=kOutput, calls=%fused_computation.31.clone.1 | convolution fusion | flops 607127040 | bytes 20971680 | tf_op jit(solution)/shard_map/while/body/eval_jaxpr/dot_general | solution.py:162
  361.8 9.9 %copy.124 = f32[4,8,128,4,128]{4,3,2,1,0:T(4,128)} copy(f32[4,8,128,4,128]{2,4,1,3,0:T(8,128)} %fusion.116) | data formatting | bytes 16777216 | tf_op jit(solution)/shard_map/while/body/eval_jaxpr/bhqek,bqhd->bekhd/transpose | solution.py:154
  371.7 9.0 %reshape.299 = f32[32,65536]{1,0:T(8,128)} reshape(f32[4,8,128,4,128]{4,3,2,1,0:T(4,128)} %copy.124) | data formatting | bytes 16777216 | tf_op jit(solution)/shard_map/while/body/eval_jaxpr/reshape | solution.py:166
  380.7 9.2 %convolution_add_fusion.6 = f32[24,65536]{1,0:T(8,128)} fusion(f32[32,65536]{1,0:T(8,128)} %reshape.299, f32[24,65536]{1,0:T(8,128)} %get-tuple-element.489, pred[]{:T(512)S(6)} %compare.14, s32[32]{0:T(128)S(1)} %eq.72, pred[32]{0:T(512)(128)(4,1)S(1)} %and.73), kind=kOutput, calls=%fused_computation.30.clone.1 | convolution fusion | flops 607127040 | bytes 20971680 | tf_op jit(solution)/shard_map/while/body/eval_jaxpr/dot_general | solution.py:165
  395.5 9.9 %copy.123 = f32[4,8,128,4,128]{4,3,2,1,0:T(4,128)} copy(f32[4,8,128,4,128]{2,4,1,3,0:T(8,128)} %convolution_bitcast_fusion.3) | data formatting | bytes 16777216 | tf_op jit(solution)/shard_map/while/body/eval_jaxpr/bhqek,bqhd->bekhd/transpose | solution.py:151
  405.4 9.0 %reshape.298 = f32[32,65536]{1,0:T(8,128)} reshape(f32[4,8,128,4,128]{4,3,2,1,0:T(4,128)} %copy.123) | data formatting | bytes 16777216 | tf_op jit(solution)/shard_map/while/body/eval_jaxpr/reshape | solution.py:163
  414.4 9.0 %convolution_add_fusion.5 = f32[24,65536]{1,0:T(8,128)} fusion(f32[32,65536]{1,0:T(8,128)} %reshape.298, f32[24,65536]{1,0:T(8,128)} %get-tuple-element.488, pred[]{:T(512)S(6)} %compare.14, s32[32]{0:T(128)S(1)} %eq.72, pred[32]{0:T(512)(128)(4,1)S(1)} %and.73), kind=kOutput, calls=%fused_computation.31.clone.1 | convolution fusion | flops 607127040 | bytes 20971680 | tf_op jit(solution)/shard_map/while/body/eval_jaxpr/dot_general | solution.py:162
  460.6 9.9 %copy.124 = f32[4,8,128,4,128]{4,3,2,1,0:T(4,128)} copy(f32[4,8,128,4,128]{2,4,1,3,0:T(8,128)} %fusion.116) | data formatting | bytes 16777216 | tf_op jit(solution)/shard_map/while/body/eval_jaxpr/bhqek,bqhd->bekhd/transpose | solution.py:154
  470.5 9.0 %reshape.299 = f32[32,65536]{1,0:T(8,128)} reshape(f32[4,8,128,4,128]{4,3,2,1,0:T(4,128)} %copy.124) | data formatting | bytes 16777216 | tf_op jit(solution)/shard_map/while/body/eval_jaxpr/reshape | solution.py:166
  479.6 9.2 %convolution_add_fusion.6 = f32[24,65536]{1,0:T(8,128)} fusion(f32[32,65536]{1,0:T(8,128)} %reshape.299, f32[24,65536]{1,0:T(8,128)} %get-tuple-element.489, pred[]{:T(512)S(6)} %compare.14, s32[32]{0:T(128)S(1)} %eq.72, pred[32]{0:T(512)(128)(4,1)S(1)} %and.73), kind=kOutput, calls=%fused_computation.30.clone.1 | convolution fusion | flops 607127040 | bytes 20971680 | tf_op jit(solution)/shard_map/while/body/eval_jaxpr/dot_general | solution.py:165
  494.4 9.9 %copy.123 = f32[4,8,128,4,128]{4,3,2,1,0:T(4,128)} copy(f32[4,8,128,4,128]{2,4,1,3,0:T(8,128)} %convolution_bitcast_fusion.3) | data formatting | bytes 16777216 | tf_op jit(solution)/shard_map/while/body/eval_jaxpr/bhqek,bqhd->bekhd/transpose | solution.py:151
  504.3 9.0 %reshape.298 = f32[32,65536]{1,0:T(8,128)} reshape(f32[4,8,128,4,128]{4,3,2,1,0:T(4,128)} %copy.123) | data formatting | bytes 16777216 | tf_op jit(solution)/shard_map/while/body/eval_jaxpr/reshape | solution.py:163
  513.3 9.0 %convolution_add_fusion.5 = f32[24,65536]{1,0:T(8,128)} fusion(f32[32,65536]{1,0:T(8,128)} %reshape.298, f32[24,65536]{1,0:T(8,128)} %get-tuple-element.488, pred[]{:T(512)S(6)} %compare.14, s32[32]{0:T(128)S(1)} %eq.72, pred[32]{0:T(512)(128)(4,1)S(1)} %and.73), kind=kOutput, calls=%fused_computation.31.clone.1 | convolution fusion | flops 607127040 | bytes 20971680 | tf_op jit(solution)/shard_map/while/body/eval_jaxpr/dot_general | solution.py:162
  559.5 9.9 %copy.124 = f32[4,8,128,4,128]{4,3,2,1,0:T(4,128)} copy(f32[4,8,128,4,128]{2,4,1,3,0:T(8,128)} %fusion.116) | data formatting | bytes 16777216 | tf_op jit(solution)/shard_map/while/body/eval_jaxpr/bhqek,bqhd->bekhd/transpose | solution.py:154
  569.4 9.0 %reshape.299 = f32[32,65536]{1,0:T(8,128)} reshape(f32[4,8,128,4,128]{4,3,2,1,0:T(4,128)} %copy.124) | data formatting | bytes 16777216 | tf_op jit(solution)/shard_map/while/body/eval_jaxpr/reshape | solution.py:166
  578.4 9.2 %convolution_add_fusion.6 = f32[24,65536]{1,0:T(8,128)} fusion(f32[32,65536]{1,0:T(8,128)} %reshape.299, f32[24,65536]{1,0:T(8,128)} %get-tuple-element.489, pred[]{:T(512)S(6)} %compare.14, s32[32]{0:T(128)S(1)} %eq.72, pred[32]{0:T(512)(128)(4,1)S(1)} %and.73), kind=kOutput, calls=%fused_computation.30.clone.1 | convolution fusion | flops 607127040 | bytes 20971680 | tf_op jit(solution)/shard_map/while/body/eval_jaxpr/dot_general | solution.py:165
  593.2 9.9 %copy.123 = f32[4,8,128,4,128]{4,3,2,1,0:T(4,128)} copy(f32[4,8,128,4,128]{2,4,1,3,0:T(8,128)} %convolution_bitcast_fusion.3) | data formatting | bytes 16777216 | tf_op jit(solution)/shard_map/while/body/eval_jaxpr/bhqek,bqhd->bekhd/transpose | solution.py:151
  603.1 9.0 %reshape.298 = f32[32,65536]{1,0:T(8,128)} reshape(f32[4,8,128,4,128]{4,3,2,1,0:T(4,128)} %copy.123) | data formatting | bytes 16777216 | tf_op jit(solution)/shard_map/while/body/eval_jaxpr/reshape | solution.py:163
  612.2 9.0 %convolution_add_fusion.5 = f32[24,65536]{1,0:T(8,128)} fusion(f32[32,65536]{1,0:T(8,128)} %reshape.298, f32[24,65536]{1,0:T(8,128)} %get-tuple-element.488, pred[]{:T(512)S(6)} %compare.14, s32[32]{0:T(128)S(1)} %eq.72, pred[32]{0:T(512)(128)(4,1)S(1)} %and.73), kind=kOutput, calls=%fused_computation.31.clone.1 | convolution fusion | flops 607127040 | bytes 20971680 | tf_op jit(solution)/shard_map/while/body/eval_jaxpr/dot_general | solution.py:162
  647.9 8.4 %slice.127 = f32[16,131072]{1,0:T(8,128)} slice(f32[24,131072]{1,0:T(8,128)} %constant_dynamic-update-slice_fusion.2), slice={[3:19], [0:131072]} | slice | bytes 16777216 | tf_op jit(solution)/shard_map/slice | solution.py:187
  667.0 20.5 %scatter-add.6 = f32[16,131072]{1,0:T(8,128)} dynamic-update-slice(f32[16,131072]{1,0:T(8,128)} %slice.127, f32[3,131072]{1,0:T(4,128)S(1)} %convert_add_fusion, s32[]{:T(128)} %constant.123.clone.1, s32[]{:T(128)} %constant.123.clone.1) | dynamic-update-slice | bytes 3145732 | tf_op jit(solution)/shard_map/scatter-add | solution.py:190
  691.8 13.4 %scatter-add.9 = f32[16,131072]{1,0:T(8,128)} dynamic-update-slice(f32[16,131072]{1,0:T(8,128)} %scatter-add.6, f32[3,131072]{1,0:T(4,128)S(1)} %slice_add_fusion, s32[]{:T(128)} %constant.133.clone.1, s32[]{:T(128)} %constant.123.clone.1) | dynamic-update-slice | bytes 3145732 | tf_op jit(solution)/shard_map/scatter-add | solution.py:191
  705.2 9.9 %all-reduce.3.cloned.1.call-done = f32[2,131072]{1,0:T(2,128)} async-done(((f32[2,131072]{1,0:T(2,128)}), f32[2,131072]{1,0:T(2,128)}) %all-reduce.3.cloned.1.call-update) | async-done | bytes 1048592 | tf_op jit(solution)/shard_map/psum | solution.py:192
  (241 shorter events, 395.9 us)
Async XLA Ops:
  7.2 3.3 copy-start.7
  7.2 85.5 %all-gather.4.cloned.1.call-start = ((), (), s32[]{:S(2)}) async-start(), calls=%async_computation.1 | async-start | bytes 2621440 | tf_op jit(solution)/shard_map/all_gather | solution.py:85
  11.9 4.8 copy-start.11
  16.8 6.7 copy-start.9
  16.8 13.0 %copy-start.8 = (s32[64,6]{0,1:T(8,128)S(1)}, s32[64,6]{0,1:T(8,128)}, u32[]{:S(2)}) copy-start(s32[64,6]{0,1:T(8,128)} %param.19) | copy-start | bytes 4612
  16.8 13.3 %copy-start.6 = (bf16[2048,512]{1,0:T(8,128)(2,1)S(1)}, bf16[2048,512]{1,0:T(8,128)(2,1)}, u32[]{:S(2)}) copy-start(bf16[2048,512]{1,0:T(8,128)(2,1)} %param.17) | copy-start | bytes 6291460
  20.8 694.4 %all-reduce.3.cloned.1.call-start = ((), (), s32[]{:S(2)}) async-start(), calls=%async_computation | async-start | bytes 2097152 | tf_op jit(solution)/shard_map/psum | solution.py:192
  23.5 36.7 %collective-permute-start = (bf16[384,1024]{1,0:T(8,128)(2,1)}, bf16[384,1024]{1,0:T(8,128)(2,1)S(1)}, u32[]{:S(2)}, u32[]{:S(2)}) collective-permute-start(bf16[384,1024]{1,0:T(8,128)(2,1)} %get-tuple-element.302), channel_id=1, source_target_pairs={{0,8},{8,16},{16,24},{1,9},{9,17},{17,25},{2,10},{10,18},{18,26},{... | collective-permute-start | bytes 2359304 | tf_op jit(solution)/shard_map/ppermute | solution.py:21
  28.5 54.8 %collective-permute-start.1 = (bf16[384,1024]{1,0:T(8,128)(2,1)}, bf16[384,1024]{1,0:T(8,128)(2,1)}, u32[]{:S(2)}, u32[]{:S(2)}) collective-permute-start(bf16[384,1024]{1,0:T(8,128)(2,1)} %get-tuple-element.303), channel_id=1, source_target_pairs={{8,0},{16,8},{24,16},{9,1},{17,9},{25,17},{10,2},{18,10},{26,18},{... | collective-permute-start | bytes 2359304 | tf_op jit(solution)/shard_map/ppermute | solution.py:23
  132.0 2.2 copy-start.3
  206.6 2.2 copy-start.3
  250.9 3.7 copy-start.4
  250.9 3.8 copy-start.5
  254.6 3.5 copy-start
  283.8 8.3 %copy-start.2 = (bf16[4,4,128,8,128]{4,2,3,1,0:T(8,128)(2,1)S(1)}, bf16[4,4,128,8,128]{4,2,3,1,0:T(8,128)(2,1)}, u32[]{:S(2)}) copy-start(bf16[4,4,128,8,128]{4,2,3,1,0:T(8,128)(2,1)} %copy-done.1) | copy-start | bytes 12582916 | tf_op jit(solution)/shard_map/while
  347.8 3.7 copy-start.4
  347.8 3.8 copy-start.5
  351.6 3.5 copy-start
  380.7 9.2 %copy-start.2 = (bf16[4,4,128,8,128]{4,2,3,1,0:T(8,128)(2,1)S(1)}, bf16[4,4,128,8,128]{4,2,3,1,0:T(8,128)(2,1)}, u32[]{:S(2)}) copy-start(bf16[4,4,128,8,128]{4,2,3,1,0:T(8,128)(2,1)} %copy-done.1) | copy-start | bytes 12582916 | tf_op jit(solution)/shard_map/while
  446.7 3.7 copy-start.4
  446.7 3.8 copy-start.5
  450.4 3.5 copy-start
  479.6 9.2 %copy-start.2 = (bf16[4,4,128,8,128]{4,2,3,1,0:T(8,128)(2,1)S(1)}, bf16[4,4,128,8,128]{4,2,3,1,0:T(8,128)(2,1)}, u32[]{:S(2)}) copy-start(bf16[4,4,128,8,128]{4,2,3,1,0:T(8,128)(2,1)} %copy-done.1) | copy-start | bytes 12582916 | tf_op jit(solution)/shard_map/while
  545.5 3.7 copy-start.4
  545.5 3.8 copy-start.5
  549.3 3.5 copy-start
  578.4 9.2 %copy-start.2 = (bf16[4,4,128,8,128]{4,2,3,1,0:T(8,128)(2,1)S(1)}, bf16[4,4,128,8,128]{4,2,3,1,0:T(8,128)(2,1)}, u32[]{:S(2)}) copy-start(bf16[4,4,128,8,128]{4,2,3,1,0:T(8,128)(2,1)} %copy-done.1) | copy-start | bytes 12582916 | tf_op jit(solution)/shard_map/while
  621.4 6.1 slice-start
  621.4 6.1 slice-start.1
  637.9 25.0 %collective-permute-start.2 = (bf16[3,131072]{1,0:T(4,128)(2,1)}, bf16[3,131072]{1,0:T(4,128)(2,1)S(1)}, u32[]{:S(2)}, u32[]{:S(2)}) collective-permute-start(bf16[3,131072]{1,0:T(4,128)(2,1)} %get-tuple-element.296), channel_id=1, source_target_pairs={{0,8},{8,16},{16,24},{1,9},{9,17},{17,25},{2,10},{10,18},{18,26},{... | collective-permute-start | bytes 2359304 | tf_op jit(solution)/shard_map/ppermute | solution.py:21
  639.9 22.9 %collective-permute-start.3 = (bf16[3,131072]{1,0:T(4,128)(2,1)}, bf16[3,131072]{1,0:T(4,128)(2,1)}, u32[]{:S(2)}, u32[]{:S(2)}) collective-permute-start(bf16[3,131072]{1,0:T(4,128)(2,1)} %get-tuple-element.297), channel_id=1, source_target_pairs={{8,0},{16,8},{24,16},{9,1},{17,9},{25,17},{10,2},{18,10},{26,18},{... | collective-permute-start | bytes 2359304 | tf_op jit(solution)/shard_map/ppermute | solution.py:23
  691.8 23.4 %copy-start.10 = (s32[2]{0:T(128)S(1)}, s32[2]{0:T(128)}, u32[]{:S(2)}) copy-start(s32[2]{0:T(128)} %copy-done.9) | copy-start | bytes 28
  (6 other events, 13.1 us)
Sparse Core Ops, SparseCore 0:
  20.9 63.6 all-gather.3
  662.9 52.1 all-reduce.2
